TPU v7x, 512 devices: a whole 4x4x16 slice. The times are simulated.
512 devices in a mesh: grp: 16 (over y_lo, x, core), mem: 32 (over y_hi, z).
Axes of the slice: x: 4, y: 4 (y_hi: 2, y_lo: 2; y = y_hi * 2 + y_lo), z: 16, core: 2. Of those that a mesh axis runs over, the one named last changes fastest.
Arguments:
- features: float32 [12288, 256], P('mem'), may hold values from -6 to 6
- patterns: bfloat16 [16, 32, 32, 2, 128, 128], P('grp', 'mem'), may hold values from 0 to 2, as said below
- src_tile: int32 [16, 32, 32, 2], P('grp', 'mem'), may hold values from 0 to 2
- dst_tile: int32 [16, 32, 32, 2], P('grp', 'mem'), may hold values from 0 to 2
- tile_count: int32 [16, 32], P('grp', 'mem'), may hold values from 16 to 64, as said below
- cotangent: float32 [12288, 256], P(('mem', 'grp')), may hold values from -6 to 6
- w_self: float32 [256, 256], replicated, may hold values from -0.375 to 0.375
- w_neigh: float32 [256, 256], replicated, may hold values from -0.375 to 0.375
- bias: float32 [256], replicated, may hold values from -3 to 3
Outputs:
- layer_out: float32 [12288, 256], P(('mem', 'grp'))
- grad_self: float32 [256, 256], replicated
- grad_neigh: float32 [256, 256], replicated
- grad_bias: float32 [256], replicated
Inputs may be any that keep to these rules, and one draw needn't show every extreme that they name: `tile_count`: some group has all 64 slots live for some destination block. `patterns`: edge weights are zero or positive.
All inputs are finite; a program needn't handle non-finite values.
Results may differ from a plain program's by a relative error of at most 0.0003.
Values sent between devices are 32-bit elements; how exact they have to be, the bound alone decides.
A program may use at most 64 MiB of HBM per device.

v0:
```python
import jax
import jax.numpy as jnp
from jax import lax
from jax.sharding import PartitionSpec as P


def accumulate(masks, place, rows):
    contrib = jnp.einsum("jpab,jpbd->jpad", masks, rows, precision=lax.Precision.HIGHEST)
    return jnp.einsum("jpt,jpad->tad", place, contrib, precision=lax.Precision.HIGHEST)


def finish(summed, degree, own, cotangent, w_self, w_neigh, bias):
    neigh = summed / jnp.sqrt(1.0 + degree)[:, None]
    pre = jnp.dot(own, w_self, precision=lax.Precision.HIGHEST, preferred_element_type=jnp.float32)
    pre = (
        pre
        + jnp.dot(
            neigh, w_neigh, precision=lax.Precision.HIGHEST, preferred_element_type=jnp.float32
        )
        + bias
    )
    sig = jax.nn.sigmoid(pre)
    layer_out = pre * sig
    dpre = cotangent * sig * (1.0 + pre * (1.0 - sig))
    grad_self = jnp.dot(
        own.T, dpre, precision=lax.Precision.HIGHEST, preferred_element_type=jnp.float32
    )
    grad_neigh = jnp.dot(
        neigh.T, dpre, precision=lax.Precision.HIGHEST, preferred_element_type=jnp.float32
    )
    return (layer_out, grad_self, grad_neigh, jnp.sum(dpre, axis=0))


def on_device(features, patterns, src_tile, dst_tile, tile_count, cotangent, w_self, w_neigh, bias):
    weights = patterns[0, 0]
    sources = src_tile[0, 0]
    targets = dst_tile[0, 0]
    tile = weights.shape[2]
    members = weights.shape[0]
    slots = weights.shape[1]
    block = features.shape[0]
    width = features.shape[1]
    tblocks = block // tile
    order = jnp.arange(members)[:, None] * slots + jnp.arange(slots)[None, :]
    live = (order < tile_count[0, 0]).astype(jnp.float32)
    place = (targets[..., None] == jnp.arange(tblocks)).astype(jnp.float32) * live[..., None]
    masks = weights.astype(jnp.float32)
    degree = jnp.einsum(
        "jpt,jpa->ta", place, jnp.sum(masks, axis=3), precision=lax.Precision.HIGHEST
    ).reshape(block)
    piece = lax.all_gather(features, "mem", axis=0, tiled=True)
    shards = piece.shape[0] // block
    stacked = piece.reshape(shards * tblocks, tile, width)
    picked = jnp.arange(shards)[:, None] * tblocks + sources
    summed = accumulate(masks, place, stacked[picked])
    summed = summed.reshape(block, width)
    share = cotangent.shape[0]
    offset = lax.axis_index("grp") * share
    own = lax.dynamic_slice_in_dim(features, offset, share, 0)
    part_sum, part_degree = (
        lax.psum_scatter(summed, "grp", scatter_dimension=0, tiled=True),
        lax.psum_scatter(degree, "grp", scatter_dimension=0, tiled=True),
    )
    layer_out, grad_self, grad_neigh, grad_bias = finish(
        part_sum, part_degree, own, cotangent, w_self, w_neigh, bias
    )
    grad_self, grad_neigh, grad_bias = lax.psum((grad_self, grad_neigh, grad_bias), ("grp", "mem"))
    return (layer_out, grad_self, grad_neigh, grad_bias)


def solution(mesh):
    placed = (
        P("mem", None),
        P("grp", "mem", None, None, None, None),
        P("grp", "mem", None, None),
        P("grp", "mem", None, None),
        P("grp", "mem"),
        P(("mem", "grp"), None),
        P(),
        P(),
        P(),
    )
    return jax.shard_map(
        on_device,
        mesh=mesh,
        in_specs=placed,
        out_specs=(P(("mem", "grp"), None), P(), P(), P()),
        check_vma=False,
    )
```

profile of v0, /device:TPU:1, one launch (start us, length us, event | category | flops | bytes accessed | tf_op | source)
XLA Modules:
  0.0 824.0 jit_solution(17553899040861458311)
XLA Ops:
  7.2 0.7 all-gather.2.cloned.1.call-update
  8.6 0.7 compare_select_fusion
  9.3 0.1 copy.16
  9.4 0.1 reshape.97
  9.5 227.4 %all-gather.2.cloned.1.call-done = f32[12288,256]{1,0:T(8,128)} async-done(((f32[384,256]{1,0:T(8,128)}), f32[12288,256]{1,0:T(8,128)}) %all-gather.2.cloned.1.call-update) | async-done | bytes 12582928 | tf_op jit(solution)/shard_map/all_gather | solution.py:51
  236.9 9.0 %gather_fusion = f32[64,128,256]{2,1,0:T(8,128)} fusion(f32[96,128,256]{2,1,0:T(8,128)} %bitcast.37, s32[1024]{0:T(1024)S(1)} %pad_clamp_fusion), kind=kCustom, calls=%fused_computation | custom fusion | bytes 16777472 | tf_op jit(solution)/shard_map/gather | solution.py:55
  246.0 11.7 %convolution_bitcast_fusion = f32[32,2,128,256]{2,3,1,0:T(8,128)} fusion(f32[32,2,128,256]{3,2,1,0:T(8,128)} %bitcast.36, bf16[1,1,32,2,128,128]{5,4,3,2,1,0:T(8,128)(2,1)S(1)} %copy-done.1), kind=kOutput, calls=%fused_computation.2 | convolution fusion | flops 3221225472 | bytes 18874368 | tf_op jit(solution)/shard_map/jpab,jpbd->jpad/dot_general | solution.py:8
  257.7 10.4 %copy.18 = f32[32,2,128,256]{3,0,1,2:T(8,128)} copy(f32[32,2,128,256]{2,3,1,0:T(8,128)} %convolution_bitcast_fusion) | data formatting | bytes 16777216 | tf_op jit(solution)/shard_map/jpab,jpbd->jpad/dot_general | solution.py:8
  268.0 6.6 convolution_bitcast_fusion.1
  274.6 0.8 copy.19
  275.5 1.3 dynamic-slice
  277.4 0.6 convert_reduce_fusion
  278.1 0.2 convolution_bitcast_fusion.2
  278.3 31.2 %all-reduce = f32[384]{0:T(512)S(1)} all-reduce(f32[384]{0:T(512)S(1)} %convolution_bitcast_fusion.2), channel_id=3, replica_groups=mesh['grp'=16,'mem'=32] {'grp'}, use_global_device_ids=true, to_apply=%region_2.0.clone | all-reduce | flops 384 | bytes 3072
  309.5 0.1 fusion.16
  309.6 1.0 fusion.6
  310.5 30.5 %reduce-scatter.2.cloned.1.call-done = f32[24,256]{1,0:T(8,128)} async-done(((f32[384,256]{1,0:T(8,128)}), f32[24,256]{1,0:T(8,128)}) %reduce-scatter.2.cloned.1.call-update) | async-done | bytes 24592 | tf_op jit(solution)/shard_map/reduce_scatter | solution.py:61
  341.0 1.6 fusion.21
  342.7 1.9 fusion.4
  344.5 1.9 fusion.9
  346.5 106.5 %psum.23 = f32[256]{0:T(256)} all-reduce(f32[256]{0:T(256)S(1)} %get-tuple-element.6), channel_id=1, replica_groups=mesh['grp'=16,'mem'=32] {'grp','mem'}, use_global_device_ids=true, to_apply=%region_6.0 | all-reduce | flops 256 | bytes 2048 | tf_op jit(solution)/shard_map/psum | solution.py:67
  452.9 361.2 %all-reduce.4.cloned.1.call-done = (f32[256,256]{1,0:T(8,128)}, f32[256,256]{1,0:T(8,128)}) async-done(((f32[256,256]{1,0:T(8,128)}, f32[256,256]{1,0:T(8,128)}), (f32[256,256]{1,0:T(8,128)}, f32[256,256]{1,0:T(8,128)})) %all-reduce.4.cloned.1.call-update) | async-done | bytes 524304 | tf_op jit(solution)/shard_map/psum | solution.py:67
  814.1 1.7 copy.27
  815.8 1.7 copy.28
  (21 shorter events, 0.2 us)
Async XLA Ops:
  7.2 333.9 %copy-start = (f32[256,256]{1,0:T(8,128)S(1)}, f32[256,256]{1,0:T(8,128)}, u32[]{:S(2)}) copy-start(f32[256,256]{1,0:T(8,128)} %param.16) | copy-start | bytes 786436
  7.2 229.8 %all-gather.2.cloned.1.call-start = ((), (), s32[]{:S(2)}) async-start(), calls=%async_computation.1 | async-start | bytes 12976128 | tf_op jit(solution)/shard_map/all_gather | solution.py:51
  7.9 333.1 %reduce-scatter.2.cloned.1.call-start = ((), (), s32[]{:S(2)}) async-start(), calls=%async_computation.2 | async-start | bytes 417792 | tf_op jit(solution)/shard_map/reduce_scatter | solution.py:61
  236.9 9.0 %copy-start.1 = (bf16[1,1,32,2,128,128]{5,4,3,2,1,0:T(8,128)(2,1)S(1)}, bf16[1,1,32,2,128,128]{5,4,3,2,1,0:T(8,128)(2,1)}, u32[]{:S(2)}) copy-start(bf16[1,1,32,2,128,128]{5,4,3,2,1,0:T(8,128)(2,1)} %param.10) | copy-start | bytes 6291460
  257.6 10.4 %copy-start.4 = (s32[1,1,32,2]{2,3,1,0:T(2,128)S(1)}, s32[1,1,32,2]{2,3,1,0:T(2,128)}, u32[]{:S(2)}) copy-start(s32[1,1,32,2]{2,3,1,0:T(2,128)} %param.12) | copy-start | bytes 772
  268.0 41.5 %copy-start.2 = (f32[256,256]{1,0:T(8,128)S(1)}, f32[256,256]{1,0:T(8,128)}, u32[]{:S(2)}) copy-start(f32[256,256]{1,0:T(8,128)} %param.15) | copy-start | bytes 786436
  268.0 73.0 %copy-start.3 = (f32[24,256]{1,0:T(8,128)S(1)}, f32[24,256]{1,0:T(8,128)}, u32[]{:S(2)}) copy-start(f32[24,256]{1,0:T(8,128)} %param.14) | copy-start | bytes 73732
  268.0 73.0 %copy-start.5 = (f32[256]{0:T(256)S(1)}, f32[256]{0:T(256)}, u32[]{:S(2)}) copy-start(f32[256]{0:T(256)} %param.17) | copy-start | bytes 3076
  275.4 538.7 %all-reduce.4.cloned.1.call-start = ((), (), s32[]{:S(2)}) async-start(), calls=%async_computation.3 | async-start | bytes 1048576 | tf_op jit(solution)/shard_map/psum | solution.py:67
Sparse Core Ops, SparseCore 0:
  11.1 225.7 all-gather.1
  275.5 65.4 reduce-scatter.1
  347.1 466.9 all-reduce.3
where the time goes:
time: 825 us; the launch traced here: 824 us
  waiting for transfers between devices  620 us (75%)
  blocking collectives  138 us (17%)
  local copies, waits for them, and re-layouts  25 us (3%)
  matrix products  24.9 us (3%)
  between operations  15.1 us (2%)
    psum x1, waiting for transfers between devices, on_device(): lax.psum((grad_self, grad_neigh, grad_bias), ('grp', 'mem'))  361 us
    all_gather x1, waiting for transfers between devices, on_device(): piece = lax.all_gather(features, 'mem', axis=0, tiled=True)  227 us
    psum x1, blocking collectives, on_device(): lax.psum((grad_self, grad_neigh, grad_bias), ('grp', 'mem'))  106 us
    unnamed x1, blocking collectives  31.2 us
    reduce_scatter x1, waiting for transfers between devices, on_device(): lax.psum_scatter(summed, 'grp', scatter_dimension=0, tiled=True)  30.5 us
  transfers between devices with their start and end apart: 3, of which 3 were waited for; matrix products, arithmetic and copies ran while one was open for 0% of the time, Pallas kernels for 0%

commit v1 on v0

--- a/solution.py
+++ b/solution.py
@@ -48,7 +48,9 @@
     degree = jnp.einsum(
         "jpt,jpa->ta", place, jnp.sum(masks, axis=3), precision=lax.Precision.HIGHEST
     ).reshape(block)
-    piece = lax.all_gather(features, "mem", axis=0, tiled=True)
+    piece = jnp.concatenate(
+        lax.all_to_all(jnp.stack([features] * lax.axis_size("mem")), "mem", 0, 0), axis=0
+    )
     shards = piece.shape[0] // block
     stacked = piece.reshape(shards * tblocks, tile, width)
     picked = jnp.arange(shards)[:, None] * tblocks + sources

time: 825 us -> 1170 us (1.42)
  waiting for transfers between devices: 620 us -> 939 us
  starting transfers between devices: 0.12 us -> 19 us
    all_to_all x0 -> x1, waiting for transfers between devices: none -> 544 us  [on_device(): lax.all_to_all(jnp.stack([features] * lax.axis_size('mem')), 'mem', 0, 0)]
    all_gather x1 -> x0, waiting for transfers between devices: 227 us -> none  [on_device(): piece = lax.all_gather(features, 'mem', axis=0, tiled=True)]
    all_to_all x0 -> x1, starting transfers between devices: none -> 18.9 us  [on_device(): lax.all_to_all(jnp.stack([features] * lax.axis_size('mem')), 'mem', 0, 0)]
where the time goes in v1:
time: 1170 us
  waiting for transfers between devices  939 us (80%)
  blocking collectives  135 us (12%)
  local copies, waits for them, and re-layouts  31.9 us (3%)
  matrix products  24.8 us (2%)
  starting transfers between devices  19 us (2%)
  between operations  15.4 us (1%)
    all_to_all x1, waiting for transfers between devices, on_device(): lax.all_to_all(jnp.stack([features] * lax.axis_size('mem')), 'mem', 0, 0)  544 us
    psum x1, waiting for transfers between devices, on_device(): lax.psum((grad_self, grad_neigh, grad_bias), ('grp', 'mem'))  361 us
    psum x1, blocking collectives, on_device(): lax.psum((grad_self, grad_neigh, grad_bias), ('grp', 'mem'))  107 us
    reduce_scatter x1, waiting for transfers between devices, on_device(): lax.psum_scatter(summed, 'grp', scatter_dimension=0, tiled=True)  34.7 us
    unnamed x1, blocking collectives  27.9 us
  transfers between devices with their start and end apart: 3, of which 3 were waited for; matrix products, arithmetic and copies ran while one was open for 0% of the time, Pallas kernels for 0%

profile of v1, /device:TPU:1, one launch (start us, length us, event | category | flops | bytes accessed | tf_op | source)
XLA Modules:
  0.0 1165.9 jit_solution(10012685331903534228)
XLA Ops:
  7.2 6.9 stack.2
  14.1 18.9 %all-to-all-start = ((f32[32,384,256]{2,1,0:T(8,128)}), f32[32,384,256]{2,1,0:T(8,128)}, u32[]{:S(2)}, u32[]{:S(2)}) async-start(f32[32,384,256]{2,1,0:T(8,128)} %stack.2), calls=%async_computation | async-start | bytes 25165824 | tf_op jit(solution)/shard_map/all_to_all | solution.py:52
  33.1 0.1 copy.20
  33.2 0.1 reshape.95
  34.0 543.7 %all-to-all-done = f32[32,384,256]{2,1,0:T(8,128)} async-done(((f32[32,384,256]{2,1,0:T(8,128)}), f32[32,384,256]{2,1,0:T(8,128)}, u32[]{:S(2)}, u32[]{:S(2)}) %all-to-all-start) | async-done | bytes 12582944 | tf_op jit(solution)/shard_map/all_to_all | solution.py:52
  577.7 9.0 gather_fusion
  586.7 11.7 %convolution_bitcast_fusion = f32[32,2,128,256]{2,3,1,0:T(8,128)} fusion(f32[32,2,128,256]{3,2,1,0:T(8,128)} %bitcast.35, bf16[1,1,32,2,128,128]{5,4,3,2,1,0:T(8,128)(2,1)S(1)} %copy-done.1), kind=kOutput, calls=%fused_computation.2 | convolution fusion | flops 3221225472 | bytes 18874368 | tf_op jit(solution)/shard_map/jpab,jpbd->jpad/dot_general | solution.py:8
  598.4 10.4 copy.22
  608.8 6.6 convolution_bitcast_fusion.1
  615.3 0.8 copy.23
  616.2 1.3 dynamic-slice
  618.2 0.6 convert_reduce_fusion
  618.8 0.2 convolution_bitcast_fusion.2
  619.0 27.9 %all-reduce = f32[384]{0:T(512)S(1)} all-reduce(f32[384]{0:T(512)S(1)} %convolution_bitcast_fusion.2), channel_id=3, replica_groups=mesh['grp'=16,'mem'=32] {'grp'}, use_global_device_ids=true, to_apply=%region_2.0.clone | all-reduce | flops 384 | bytes 3072
  646.9 0.1 fusion.16
  647.0 1.0 fusion.6
  648.0 34.7 %reduce-scatter.2.cloned.1.call-done = f32[24,256]{1,0:T(8,128)} async-done(((f32[384,256]{1,0:T(8,128)}), f32[24,256]{1,0:T(8,128)}) %reduce-scatter.2.cloned.1.call-update) | async-done | bytes 24592 | tf_op jit(solution)/shard_map/reduce_scatter | solution.py:63
  682.7 1.6 fusion.21
  684.3 1.9 fusion.4
  686.1 1.9 fusion.9
  688.1 106.6 %psum.23 = f32[256]{0:T(256)} all-reduce(f32[256]{0:T(256)S(1)} %get-tuple-element.6), channel_id=1, replica_groups=mesh['grp'=16,'mem'=32] {'grp','mem'}, use_global_device_ids=true, to_apply=%region_6.0 | all-reduce | flops 256 | bytes 2048 | tf_op jit(solution)/shard_map/psum | solution.py:69
  794.7 361.0 %all-reduce.4.cloned.1.call-done = (f32[256,256]{1,0:T(8,128)}, f32[256,256]{1,0:T(8,128)}) async-done(((f32[256,256]{1,0:T(8,128)}, f32[256,256]{1,0:T(8,128)}), (f32[256,256]{1,0:T(8,128)}, f32[256,256]{1,0:T(8,128)})) %all-reduce.4.cloned.1.call-update) | async-done | bytes 524304 | tf_op jit(solution)/shard_map/psum | solution.py:69
  1155.7 1.7 copy.32
  1157.4 1.7 copy.33
  (23 shorter events, 0.2 us)
Async XLA Ops:
  7.2 675.5 %copy-start = (f32[256,256]{1,0:T(8,128)S(1)}, f32[256,256]{1,0:T(8,128)}, u32[]{:S(2)}) copy-start(f32[256,256]{1,0:T(8,128)} %param.16) | copy-start | bytes 786436
  14.1 19.0 %copy-start.6 = (s32[1,1,32,2]{2,3,1,0:T(2,128)S(1)}, s32[1,1,32,2]{2,3,1,0:T(2,128)}, u32[]{:S(2)}) copy-start(s32[1,1,32,2]{2,3,1,0:T(2,128)} %param.11) | copy-start | bytes 772
  14.1 563.6 %all-to-all-start = ((f32[32,384,256]{2,1,0:T(8,128)}), f32[32,384,256]{2,1,0:T(8,128)}, u32[]{:S(2)}, u32[]{:S(2)}) async-start(f32[32,384,256]{2,1,0:T(8,128)} %stack.2), calls=%async_computation | async-start | bytes 25165824 | tf_op jit(solution)/shard_map/all_to_all | solution.py:52
  33.0 649.6 %reduce-scatter.2.cloned.1.call-start = ((), (), s32[]{:S(2)}) async-start(), calls=%async_computation.2 | async-start | bytes 417792 | tf_op jit(solution)/shard_map/reduce_scatter | solution.py:63
  577.7 9.0 copy-start.1
  598.4 10.4 copy-start.4
  608.8 38.2 %copy-start.2 = (f32[256,256]{1,0:T(8,128)S(1)}, f32[256,256]{1,0:T(8,128)}, u32[]{:S(2)}) copy-start(f32[256,256]{1,0:T(8,128)} %param.15) | copy-start | bytes 786436
  608.8 73.9 %copy-start.3 = (f32[24,256]{1,0:T(8,128)S(1)}, f32[24,256]{1,0:T(8,128)}, u32[]{:S(2)}) copy-start(f32[24,256]{1,0:T(8,128)} %param.14) | copy-start | bytes 73732
  608.8 73.9 %copy-start.5 = (f32[256]{0:T(256)S(1)}, f32[256]{0:T(256)}, u32[]{:S(2)}) copy-start(f32[256]{0:T(256)} %param.17) | copy-start | bytes 3076
  616.2 539.6 %all-reduce.4.cloned.1.call-start = ((), (), s32[]{:S(2)}) async-start(), calls=%async_computation.3 | async-start | bytes 1048576 | tf_op jit(solution)/shard_map/psum | solution.py:69
Sparse Core Ops, SparseCore 0:
  616.3 66.2 reduce-scatter.1
  688.7 466.9 all-reduce.3
